TPU v7x, 32 devices: a whole 2x2x4 slice. The times are simulated.
32 devices in a mesh: seq: 8 (over z, x), ch: 4 (over y, core).
Axes of the slice: x: 2, y: 2, z: 4, core: 2. Of those that a mesh axis runs over, the one named last changes fastest.
Arguments:
- query_raw: bfloat16 [1024, 2048], P('seq', 'ch'), may hold values from -6 to 6
- key_raw: bfloat16 [1024, 2048], P('seq', 'ch'), may hold values from -6 to 6
- value_raw: bfloat16 [1024, 2048], P('seq', 'ch'), may hold values from -6 to 6
- featurizer: float32 [3, 7, 2048], P(None, None, 'ch'), may hold values from -2 to 2
- filter_taps: bfloat16 [1024, 2048], P(('seq', 'ch')), may hold values from -2.5 to 2.5
- cotangent: bfloat16 [1024, 2048], P('seq', 'ch'), may hold values from -6 to 6
Outputs:
- mixed: bfloat16 [1024, 2048], P('seq', 'ch')
- query_grad: bfloat16 [1024, 2048], P('seq', 'ch')
- key_grad: bfloat16 [1024, 2048], P('seq', 'ch')
- value_grad: bfloat16 [1024, 2048], P('seq', 'ch')
- filter_grad: float32 [1024, 2048], P(('seq', 'ch'))
- featurizer_grad: float32 [3, 7, 2048], P(None, None, 'ch')
All inputs are finite; a program needn't handle non-finite values.
Results may differ from a plain program's by a relative error of at most 0.0085.
Values may be sent and summed in bfloat16 or wider, within the bound.
A program may use at most 64 MiB of HBM per device.

v0:
```python
import functools
import math

import jax
import jax.numpy as jnp
import numpy as np
from jax import lax
from jax.experimental import pallas as pl
from jax.experimental.pallas import tpu as pltpu
from jax.sharding import PartitionSpec as P

TAPS = 7


exact_mode = lax.Precision.HIGHEST


def passed_along(value, axis, steps):
    count = lax.axis_size(axis)
    initial, last = (max(0, -steps), min(count, count - steps))
    return lax.ppermute(value, axis, [(source, source + steps) for source in range(initial, last)])


def spectrum_tables(half_rows, tile_width):
    full_rows = 2 * half_rows
    length_full = full_rows * tile_width
    row_index = jnp.arange(full_rows, dtype=jnp.int32)
    col_index = jnp.arange(tile_width, dtype=jnp.int32)
    outer_angle = (
        2.0
        * math.pi
        / full_rows
        * (row_index[:, None] * row_index[None, :] % full_rows).astype(jnp.float32)
    )
    twist_angle = (
        2.0
        * math.pi
        / length_full
        * (row_index[:, None] * col_index[None, :] % length_full).astype(jnp.float32)
    )
    inner_angle = (
        2.0
        * math.pi
        / tile_width
        * (col_index[:, None] * col_index[None, :] % tile_width).astype(jnp.float32)
    )
    return (
        jnp.cos(outer_angle),
        -jnp.sin(outer_angle),
        jnp.cos(twist_angle),
        -jnp.sin(twist_angle),
        jnp.cos(inner_angle),
        -jnp.sin(inner_angle),
    )


def right_product(left, table):
    return jnp.einsum("ckm,mj->ckj", left, table, precision=exact_mode)


def to_spectrum(signal, tables):
    outer_re, outer_im, twist_re, twist_im, inner_re, inner_im = tables
    half_rows = outer_re.shape[0] // 2
    tile_width = inner_re.shape[0]
    blocks = signal.reshape(signal.shape[0], half_rows, tile_width)
    section_re = jnp.einsum("kn,cnm->ckm", outer_re[:, :half_rows], blocks, precision=exact_mode)
    section_im = jnp.einsum("kn,cnm->ckm", outer_im[:, :half_rows], blocks, precision=exact_mode)
    turned_re = section_re * twist_re - section_im * twist_im
    turned_im = section_re * twist_im + section_im * twist_re
    spec_re = right_product(turned_re, inner_re) - right_product(turned_im, inner_im)
    spec_im = right_product(turned_re, inner_im) + right_product(turned_im, inner_re)
    return (spec_re, spec_im)


def from_spectrum(spectrum, tables):
    outer_re, outer_im, twist_re, twist_im, inner_re, inner_im = tables
    half_rows = outer_re.shape[0] // 2
    tile_width = inner_re.shape[0]
    spec_re, spec_im = spectrum
    back_re = right_product(spec_re, inner_re) + right_product(spec_im, inner_im)
    back_im = right_product(spec_im, inner_re) - right_product(spec_re, inner_im)
    untwist_re = back_re * twist_re + back_im * twist_im
    untwist_im = back_im * twist_re - back_re * twist_im
    signal = jnp.einsum("nk,ckm->cnm", outer_re[:half_rows], untwist_re, precision=exact_mode)
    signal = signal + jnp.einsum(
        "nk,ckm->cnm", outer_im[:half_rows], untwist_im, precision=exact_mode
    )
    return signal.reshape(signal.shape[0], half_rows * tile_width) / (2.0 * half_rows * tile_width)


def times_spectrum(first, second):
    return (
        first[0] * second[0] - first[1] * second[1],
        first[0] * second[1] + first[1] * second[0],
    )


def conj_times(first, second):
    return (
        first[0] * second[0] + first[1] * second[1],
        first[0] * second[1] - first[1] * second[0],
    )


def featurize(padded, weight, tok_rows):
    total = jnp.zeros((tok_rows, padded.shape[1]), jnp.float32)
    for lag_index in range(TAPS):
        start = TAPS - 1 - lag_index
        total = total + weight[lag_index][None, :] * padded[start : start + tok_rows]
    return total


def unfeaturize(extended, weight, tok_rows):
    total = jnp.zeros((tok_rows, extended.shape[1]), jnp.float32)
    for lag_index in range(TAPS):
        total = total + weight[lag_index][None, :] * extended[lag_index : lag_index + tok_rows]
    return total


def weight_terms(grad, padded, tok_rows):
    terms = []
    for lag_index in range(TAPS):
        start = TAPS - 1 - lag_index
        terms.append(jnp.sum(grad * padded[start : start + tok_rows], axis=0))
    return jnp.stack(terms)


def on_device_large(query_raw, key_raw, value_raw, featurizer, filter_taps, cotangent):
    tok_rows = query_raw.shape[0]
    lag_rows = TAPS - 1
    cut_start = tok_rows - lag_rows
    seq_count = lax.axis_size("seq")
    ch_count = lax.axis_size("ch")
    rim_query, rim_key, rim_value = passed_along(
        (query_raw[cut_start:], key_raw[cut_start:], value_raw[cut_start:]), "seq", 1
    )
    padded_query = jnp.concatenate([rim_query, query_raw], axis=0).astype(jnp.float32)
    padded_key = jnp.concatenate([rim_key, key_raw], axis=0).astype(jnp.float32)
    padded_value = jnp.concatenate([rim_value, value_raw], axis=0).astype(jnp.float32)
    feat_query = featurize(padded_query, featurizer[0], tok_rows)
    feat_key = featurize(padded_key, featurizer[1], tok_rows)
    feat_value = featurize(padded_value, featurizer[2], tok_rows)
    mixer = (feat_key * feat_value).astype(jnp.bfloat16)
    mix_cols = lax.all_to_all(mixer.T, "seq", split_axis=0, concat_axis=1, tiled=True)
    chan_total, row_part = (filter_taps.shape[1], filter_taps.shape[0])
    block_width = chan_total // (seq_count * ch_count)
    ordered = filter_taps.T.reshape(ch_count, seq_count, block_width, row_part)
    ordered = jnp.transpose(ordered, (1, 0, 2, 3)).reshape(chan_total, row_part)
    taps_cols = lax.all_to_all(ordered, ("seq", "ch"), split_axis=0, concat_axis=1, tiled=True)
    length_full = mix_cols.shape[1]
    tables = spectrum_tables(length_full // 128, 128)
    mix_spec = to_spectrum(mix_cols.astype(jnp.float32), tables)
    taps_spec = to_spectrum(taps_cols.astype(jnp.float32), tables)
    conv_cols = from_spectrum(times_spectrum(taps_spec, mix_spec), tables).astype(jnp.bfloat16)
    conv_rows = lax.all_to_all(conv_cols, "seq", split_axis=1, concat_axis=0, tiled=True).T
    conv_float = conv_rows.astype(jnp.float32)
    mixed = (feat_query * conv_float).astype(jnp.bfloat16)
    upstream = cotangent.astype(jnp.float32)
    gate = (upstream * feat_query).astype(jnp.bfloat16)
    gate_cols = lax.all_to_all(gate.T, "seq", split_axis=0, concat_axis=1, tiled=True)
    gate_spec = to_spectrum(gate_cols.astype(jnp.float32), tables)
    scale = length_full ** (-0.5)
    mix_grad_cols = from_spectrum(conj_times(taps_spec, gate_spec), tables).astype(jnp.bfloat16)
    taps_grad_cols = from_spectrum(conj_times(mix_spec, gate_spec), tables) * scale
    mix_back = lax.all_to_all(mix_grad_cols, "seq", split_axis=1, concat_axis=0, tiled=True)
    mix_grad_float = mix_back.T.astype(jnp.float32)
    joint_back = lax.all_to_all(
        taps_grad_cols, ("seq", "ch"), split_axis=1, concat_axis=0, tiled=True
    )
    block_width = joint_back.shape[0] // (seq_count * ch_count)
    row_part = joint_back.shape[1]
    unordered = joint_back.reshape(seq_count, ch_count, block_width, row_part)
    unordered = jnp.transpose(unordered, (1, 0, 2, 3)).reshape(joint_back.shape[0], row_part)
    filter_grad = unordered.T
    query_feat_grad = upstream * conv_float
    key_feat_grad = mix_grad_float * feat_value
    value_feat_grad = mix_grad_float * feat_key
    next_query, next_key, next_value = passed_along(
        (query_feat_grad[:lag_rows], key_feat_grad[:lag_rows], value_feat_grad[:lag_rows]),
        "seq",
        -1,
    )
    query_grad = unfeaturize(
        jnp.concatenate([query_feat_grad, next_query], axis=0), featurizer[0], tok_rows
    )
    key_grad = unfeaturize(
        jnp.concatenate([key_feat_grad, next_key], axis=0), featurizer[1], tok_rows
    )
    value_grad = unfeaturize(
        jnp.concatenate([value_feat_grad, next_value], axis=0), featurizer[2], tok_rows
    )
    partial_terms = jnp.stack(
        [
            weight_terms(query_feat_grad, padded_query, tok_rows),
            weight_terms(key_feat_grad, padded_key, tok_rows),
            weight_terms(value_feat_grad, padded_value, tok_rows),
        ]
    )
    featurizer_grad = lax.psum(partial_terms, "seq") * scale
    return (
        mixed,
        query_grad.astype(jnp.bfloat16),
        key_grad.astype(jnp.bfloat16),
        value_grad.astype(jnp.bfloat16),
        filter_grad,
        featurizer_grad,
    )


LANES = 128
HALO = 16
STEP = 32
SPLIT = (TAPS + 1) // 2
PART_ROWS = 16
MESH = pl.DeviceIdType.MESH


def angle_tables(length):
    full = 2 * length
    col = np.arange(length)
    coarse = np.arange(length // STEP + 1) * STEP
    coarse = 2.0 * np.pi / full * ((coarse[:, None] * col[None, :LANES]) % full)
    fine = 2.0 * np.pi / full * ((np.arange(STEP)[:, None] * col[None, :]) % full)
    return [
        np.asarray(part, np.float32)
        for part in (np.cos(coarse), np.sin(coarse), np.cos(fine), np.sin(fine))
    ]


def split_parts(value):
    high = value.astype(jnp.bfloat16)
    return high, (value - high.astype(jnp.float32)).astype(jnp.bfloat16)


def matmul(left, right):
    return jnp.dot(left, right, preferred_element_type=jnp.float32)


def swapped(value):
    return pltpu.roll(value, LANES // 2, axis=1)


def low_lanes(rows):
    return lax.broadcasted_iota(jnp.int32, (rows, LANES), 1) < LANES // 2


def operator_kernel(
    dims,
    q_ref, k_ref, v_ref, w_ref, taps_ref, cot_ref, ac_ref, as_ref, bc_ref, bs_ref,
    mixed_ref, qg_ref, kg_ref, vg_ref, fgrad_ref, wgrad_ref,
    ext, feat, grads, tab, taps_tx, taps_rx, mg_tx, mg_rx, taps_in, hspec, spec, conv_tx, conv_rx,
    filt_tx, filt_rx, part_tx, part_rx, sums_rx,
    halo_send, halo_recv, taps_send, taps_recv, mg_send, mg_recv,
    conv_send, conv_recv, filt_send, filt_recv, part_send, part_recv, sum_send, sum_recv,
):
    seq_count, ch_count, tok, width = dims
    count = seq_count * ch_count
    length = seq_count * tok
    tiles = width // LANES
    rows_f = length // count
    half_f = rows_f // 2
    ext_rows = tok + HALO
    f32 = jnp.float32
    seq = lax.axis_index("seq")
    ch = lax.axis_index("ch")
    me = seq * ch_count + ch
    scale = length ** (-0.5)

    def place(flat):
        return lax.div(flat, ch_count), lax.rem(flat, ch_count)

    def peer(step):
        return lax.rem(me + step, count)

    def lane_ds(tile):
        return pl.ds(pl.multiple_of(tile * LANES, LANES), LANES)

    barrier = pltpu.get_barrier_semaphore()

    @pl.loop(1, count)
    def _(step):
        pl.semaphore_signal(barrier, inc=1, device_id=place(peer(step)), device_id_type=MESH)

    low_half = low_lanes(half_f)

    @pl.loop(0, ch_count * tiles)
    def _(tile):
        cols = lane_ds(tile)
        top = taps_ref[0:half_f, cols].astype(f32)
        bottom = taps_ref[half_f:rows_f, cols].astype(f32)
        even_flat = 2 * lax.rem(tile, tiles) * ch_count + lax.div(tile, tiles)
        taps_tx[even_flat] = jnp.where(low_half, top, swapped(bottom)).astype(jnp.bfloat16)
        taps_tx[even_flat + ch_count] = jnp.where(low_half, swapped(top), bottom).astype(jnp.bfloat16)

    own = (q_ref, k_ref, v_ref, cot_ref)
    for i, ref in enumerate(own):
        ext[i, HALO : HALO + tok, :] = ref[...]

    @pl.when(seq == 0)
    def _():
        ext[:, 0:HALO, :] = jnp.zeros((4, HALO, width), jnp.bfloat16)

    @pl.when(seq == seq_count - 1)
    def _():
        ext[:, HALO + tok :, :] = jnp.zeros((4, HALO, width), jnp.bfloat16)

    def make_tables(first, last):
        @pl.loop(first, last)
        def _(a):
            rows = pl.ds(pl.multiple_of(a * STEP, STEP), STEP)
            ac = jnp.broadcast_to(ac_ref[pl.ds(a, 1), :], (STEP, LANES))
            an = jnp.broadcast_to(as_ref[pl.ds(a, 1), :], (STEP, LANES))
            for j in range(length // LANES):
                cols = slice(j * LANES, (j + 1) * LANES)
                bc, bs = bc_ref[:, cols], bs_ref[:, cols]
                tab[0, rows, cols], tab[1, rows, cols] = split_parts(ac * bc - an * bs)
                tab[2, rows, cols], tab[3, rows, cols] = split_parts(an * bc + ac * bs)

    blocks = length // STEP + 1
    early = blocks // 2
    make_tables(0, early)
    pl.semaphore_wait(barrier, count - 1)

    def halo_copy(src, dst, i, to):
        return pltpu.make_async_remote_copy(
            src_ref=src, dst_ref=dst, send_sem=halo_send.at[i], recv_sem=halo_recv.at[i],
            device_id=(to, ch), device_id_type=MESH,
        )

    def up_copy(i):
        return halo_copy(own[i].at[tok - HALO :], ext.at[i, 0:HALO], i, seq + 1)

    def down_copy(i):
        return halo_copy(own[i].at[0:HALO], ext.at[i, HALO + tok :], 3 + i, seq - 1)

    @pl.when(seq < seq_count - 1)
    def _():
        for i in range(3):
            up_copy(i).start()

    @pl.when(seq > 0)
    def _():
        for i in range(4):
            down_copy(i).start()

    def taps_copy(step):
        to_seq, to_ch = place(peer(step))
        return pltpu.make_async_remote_copy(
            src_ref=taps_tx.at[peer(step)],
            dst_ref=taps_rx.at[me], send_sem=taps_send.at[step], recv_sem=taps_recv.at[step],
            device_id=(to_seq, to_ch), device_id_type=MESH,
        )

    @pl.loop(1, count)
    def _(step):
        taps_copy(step).start()

    taps_rx[me] = taps_tx[me]

    @pl.when(seq > 0)
    def _():
        for i in range(3):
            up_copy(i).wait_recv()

    @pl.when(seq < seq_count - 1)
    def _():
        for i in range(4):
            down_copy(i).wait_recv()

    def mg_copy(to):
        return pltpu.make_async_remote_copy(
            src_ref=mg_tx.at[to], dst_ref=mg_rx.at[seq], send_sem=mg_send.at[to],
            recv_sem=mg_recv.at[seq], device_id=(to, ch), device_id_type=MESH,
        )

    low_tok = low_lanes(tok)

    @pl.loop(0, tiles)
    def _(turn):
        tile = lax.rem(turn + lax.div(seq, 2), tiles)
        cols = lane_ds(tile)
        parts = []
        for i in range(3):
            raw = ext[i, :, cols].astype(f32)
            total = jnp.zeros((ext_rows, LANES), f32)
            for lag in range(TAPS):
                total = total + w_ref[i, lag : lag + 1, cols] * raw[HALO - lag : HALO - lag + ext_rows]
            feat[i, :, cols] = total
            parts.append(total[:tok])
        mix = parts[1] * parts[2]
        gate = ext[3, HALO : HALO + tok, cols].astype(f32) * parts[0]
        even = jnp.where(low_tok, mix, swapped(gate)).astype(jnp.bfloat16)
        odd = jnp.where(low_tok, swapped(mix), gate).astype(jnp.bfloat16)
        for side, value in ((0, even), (1, odd)):
            to = 2 * tile + side
            mg_tx[to] = value

            @pl.when(to != seq)
            def _():
                mg_copy(to).start()

            @pl.when(to == seq)
            def _():
                mg_rx[to] = value

    make_tables(early, blocks)

    @pl.loop(1, count)
    def _(step):
        taps_copy(step).wait_recv()

    low_count = low_lanes(count * half_f)
    taps_all = taps_rx[...].reshape(count * half_f, LANES).astype(f32)
    taps_turned = swapped(taps_all)
    for side, pair in enumerate(((taps_all, taps_turned), (taps_turned, taps_all))):
        value = jnp.where(low_count, *pair).astype(jnp.bfloat16)
        taps_in[:, side * half_f : (side + 1) * half_f, :] = value.reshape(count, half_f, LANES)

    chunk = min(2 * LANES, length)

    def row_chunk(i):
        return pl.ds(pl.multiple_of(i * chunk, chunk), chunk)

    @pl.loop(0, length // chunk)
    def _(i):
        rows = row_chunk(i)
        hspec[0, rows, :] = matmul(tab[0, rows, :], taps_in[...].reshape(length, LANES)) + matmul(tab[1, rows, :], taps_in[...].reshape(length, LANES))
        hspec[1, rows, :] = matmul(tab[2, rows, :], taps_in[...].reshape(length, LANES)) + matmul(tab[3, rows, :], taps_in[...].reshape(length, LANES))

    def from_peer(copy_of, total, mine):
        @pl.loop(0, total)
        def _(source):
            @pl.when(source != mine)
            def _():
                copy_of(source).wait_recv()

    def mg_arrival(source):
        return pltpu.make_async_remote_copy(
            src_ref=mg_tx.at[source], dst_ref=mg_rx.at[source], send_sem=mg_send.at[source],
            recv_sem=mg_recv.at[source], device_id=(source, ch), device_id_type=MESH,
        )

    from_peer(mg_arrival, seq_count, seq)

    signals = mg_rx.at[...]
    low_chunk = low_lanes(chunk)

    @pl.loop(0, length // chunk)
    def _(i):
        rows = row_chunk(i)
        both = signals[...].reshape(length, LANES)
        xr = matmul(tab[0, rows, :], both) + matmul(tab[1, rows, :], both)
        xs = matmul(tab[2, rows, :], both) + matmul(tab[3, rows, :], both)
        bins = lax.broadcasted_iota(jnp.int32, (chunk, LANES), 0) + i * chunk
        weight = jnp.where(bins == 0, 0.5 / length, 1.0 / length)
        hr = hspec[0, rows, :]
        hs = hspec[1, rows, :]
        wr, ws = xr * weight, xs * weight
        turned = jnp.where(low_chunk, -hs, hs)
        pr = hr * wr + turned * ws
        ps = hr * ws - turned * wr
        other_r, other_s = swapped(xr), swapped(xs)
        fr = wr * other_r + ws * other_s
        fs = wr * other_s - ws * other_r
        for j, value in ((0, pr), (2, ps)):
            spec[j, rows, 0:LANES], spec[j + 1, rows, 0:LANES] = split_parts(value)
        for j, value in ((0, fr), (2, fs)):
            spec[j, rows, LANES:], spec[j + 1, rows, LANES:] = split_parts(value)

    sign_full = 1.0 - 2.0 * lax.rem(lax.broadcasted_iota(jnp.int32, (length, LANES), 0), 2).astype(f32)
    last_x = jnp.sum(mg_rx[...].reshape(length, LANES).astype(f32) * sign_full, axis=0, keepdims=True)
    last_h = jnp.sum(taps_in[...].reshape(length, LANES).astype(f32) * sign_full, axis=0, keepdims=True)
    half_weight = 0.5 / length
    last_conv = last_x * last_h * half_weight
    last_filt = last_x * swapped(jnp.broadcast_to(last_x, (8, LANES)))[0:1] * half_weight

    def conv_copy(to):
        return pltpu.make_async_remote_copy(
            src_ref=conv_tx.at[to], dst_ref=conv_rx.at[seq], send_sem=conv_send.at[to],
            recv_sem=conv_recv.at[seq], device_id=(to, ch), device_id_type=MESH,
        )

    def filt_copy(to):
        return pltpu.make_async_remote_copy(
            src_ref=filt_tx.at[to], dst_ref=filt_rx.at[me], send_sem=filt_send.at[to],
            recv_sem=filt_recv.at[me], device_id=place(to), device_id_type=MESH,
        )

    sign_ext = sign_full[:ext_rows]

    @pl.loop(0, seq_count)
    def _(turn):
        to = lax.rem(seq + 1 + turn, seq_count)
        rows = pl.ds(pl.multiple_of(to * tok, tok), ext_rows)
        out = jnp.zeros((ext_rows, 2 * LANES), f32)
        for j in (0, 2):
            high = tab[j, rows, :]
            out = out + matmul(high, spec[j]) + matmul(high, spec[j + 1]) + matmul(tab[j + 1, rows, :], spec[j])
        conv_tx[to] = (out[:, :LANES] + sign_ext * last_conv).astype(jnp.bfloat16)
        filt = (out[:, LANES:] + sign_ext * last_filt) * scale

        @pl.when(to != seq)
        def _():
            conv_copy(to).start()

        @pl.when(to == seq)
        def _():
            conv_rx[to] = conv_tx[to]

        for c in range(ch_count):
            top = filt[c * rows_f : c * rows_f + half_f]
            bottom = filt[c * rows_f + half_f : (c + 1) * rows_f]
            flat = to * ch_count + c
            filt_tx[flat] = jnp.where(low_half, top, swapped(bottom)).astype(jnp.bfloat16)


    filt_rx[me] = filt_tx[me]

    def conv_arrival(source):
        return pltpu.make_async_remote_copy(
            src_ref=conv_tx.at[source], dst_ref=conv_rx.at[source], send_sem=conv_send.at[source],
            recv_sem=conv_recv.at[source], device_id=(source, ch), device_id_type=MESH,
        )

    from_peer(conv_arrival, seq_count, seq)
    low_ext = low_lanes(ext_rows)
    row_ext = lax.broadcasted_iota(jnp.int32, (ext_rows, LANES), 0)
    keep = jnp.logical_or(row_ext < tok, seq < seq_count - 1)

    def part_copy(to):
        return pltpu.make_async_remote_copy(
            src_ref=part_tx.at[to], dst_ref=part_rx.at[seq], send_sem=part_send.at[to],
            recv_sem=part_recv.at[seq], device_id=(to, ch), device_id_type=MESH,
        )

    @pl.loop(0, tiles)
    def _(tile):
        cols = lane_ds(tile)
        first = jnp.where(keep, conv_rx[2 * tile].astype(f32), 0.0)
        second = jnp.where(keep, conv_rx[2 * tile + 1].astype(f32), 0.0)
        conv = jnp.where(low_ext, first, swapped(second))
        mix_grad = jnp.where(low_ext, swapped(first), second)
        mixed_ref[:, cols] = (feat[0, :tok, cols] * conv[:tok]).astype(jnp.bfloat16)
        terms = (
            ext[3, HALO:, cols].astype(f32) * conv,
            mix_grad * feat[2, :, cols],
            mix_grad * feat[1, :, cols],
        )
        lags = []
        for i in range(3):
            grads[i, :, cols] = terms[i]
            raw = ext[i, :, cols].astype(f32)
            sums = [
                jnp.sum(terms[i][:tok] * raw[HALO - lag : HALO - lag + tok], axis=0, keepdims=True)
                for lag in range(TAPS)
            ]
            lags.append(sums)
        for side in range(2):
            picked = [row for sums in lags for row in sums[side * SPLIT : (side + 1) * SPLIT]]
            picked.append(jnp.zeros((PART_ROWS - len(picked), LANES), f32))
            to = 2 * tile + side
            part_tx[to] = jnp.concatenate(picked, axis=0)

            @pl.when(to != seq)
            def _():
                part_copy(to).start()

            @pl.when(to == seq)
            def _():
                part_rx[to] = part_tx[to]

    @pl.loop(1, count)
    def _(step):
        filt_copy(peer(step)).start()

    @pl.loop(0, tiles)
    def _(tile):
        cols = lane_ds(tile)
        for i, ref in enumerate((qg_ref, kg_ref, vg_ref)):
            term = grads[i, :, cols]
            total = jnp.zeros((tok, LANES), f32)
            for lag in range(TAPS):
                total = total + w_ref[i, lag : lag + 1, cols] * term[lag : lag + tok]
            ref[:, cols] = total.astype(jnp.bfloat16)

    def part_arrival(source):
        return pltpu.make_async_remote_copy(
            src_ref=part_tx.at[source], dst_ref=part_rx.at[source], send_sem=part_send.at[source],
            recv_sem=part_recv.at[source], device_id=(source, ch), device_id_type=MESH,
        )

    from_peer(part_arrival, seq_count, seq)
    own_sum = part_rx[0]
    for source in range(1, seq_count):
        own_sum = own_sum + part_rx[source]
    sums_rx[seq] = own_sum * scale

    def sum_copy(to):
        return pltpu.make_async_remote_copy(
            src_ref=sums_rx.at[seq], dst_ref=sums_rx.at[seq], send_sem=sum_send.at[to],
            recv_sem=sum_recv.at[seq], device_id=(to, ch), device_id_type=MESH,
        )

    @pl.loop(1, seq_count)
    def _(step):
        sum_copy(lax.rem(seq + step, seq_count)).start()

    def filt_arrival(source):
        return pltpu.make_async_remote_copy(
            src_ref=filt_tx.at[source], dst_ref=filt_rx.at[source], send_sem=filt_send.at[source],
            recv_sem=filt_recv.at[source], device_id=place(source), device_id_type=MESH,
        )

    from_peer(filt_arrival, count, me)

    @pl.loop(0, ch_count * tiles)
    def _(tile):
        cols = lane_ds(tile)
        pair = lax.rem(tile, tiles)
        owner = lax.div(tile, tiles)
        first = filt_rx[2 * pair * ch_count + owner].astype(f32)
        second = filt_rx[(2 * pair + 1) * ch_count + owner].astype(f32)
        fgrad_ref[0:half_f, cols] = jnp.where(low_half, first, swapped(second))
        fgrad_ref[half_f:rows_f, cols] = jnp.where(low_half, swapped(first), second)

    def sum_arrival(source):
        return pltpu.make_async_remote_copy(
            src_ref=sums_rx.at[seq], dst_ref=sums_rx.at[source], send_sem=sum_send.at[source],
            recv_sem=sum_recv.at[source], device_id=(source, ch), device_id_type=MESH,
        )

    from_peer(sum_arrival, seq_count, seq)
    for tile in range(tiles):
        cols = slice(tile * LANES, (tile + 1) * LANES)
        for side in range(2):
            rows = min(SPLIT, TAPS - side * SPLIT)
            for i in range(3):
                wgrad_ref[i, side * SPLIT : side * SPLIT + rows, cols] = sums_rx[
                    2 * tile + side, i * rows : (i + 1) * rows
                ]

    @pl.when(seq < seq_count - 1)
    def _():
        for i in range(3):
            up_copy(i).wait_send()

    @pl.when(seq > 0)
    def _():
        for i in range(4):
            down_copy(i).wait_send()

    @pl.loop(1, count)
    def _(step):
        taps_copy(step).wait_send()
        filt_copy(peer(step)).wait_send()

    @pl.loop(1, seq_count)
    def _(step):
        to = lax.rem(seq + step, seq_count)
        mg_copy(to).wait_send()
        conv_copy(to).wait_send()
        part_copy(to).wait_send()
        sum_copy(to).wait_send()


def write_out(*refs):
    half = len(refs) // 2
    for source, target in zip(refs[:half], refs[half:]):
        target[...] = source[...]


def on_device(dims, *args):
    seq_count, ch_count, tok, width = dims
    count = seq_count * ch_count
    length = seq_count * tok
    half_f = length // count // 2
    bf16, f32 = jnp.bfloat16, jnp.float32
    vmem = pl.BlockSpec(memory_space=pltpu.VMEM)
    ext_rows = tok + HALO
    dma = pltpu.SemaphoreType.DMA
    out = jax.ShapeDtypeStruct((tok, width), bf16)
    outs = (
        out, out, out, out,
        jax.ShapeDtypeStruct((length // count, width * ch_count), f32),
        jax.ShapeDtypeStruct((3, TAPS, width), f32),
    )
    results = pl.pallas_call(
        functools.partial(operator_kernel, dims),
        out_shape=outs,
        in_specs=[vmem] * 10,
        out_specs=(vmem,) * 6,
        scratch_shapes=[
            pltpu.VMEM((4, tok + 2 * HALO, width), bf16),
            pltpu.VMEM((3, ext_rows, width), f32),
            pltpu.VMEM((3, ext_rows, width), f32),
            pltpu.VMEM((4, length + STEP, length), bf16),
            pltpu.VMEM((count, half_f, LANES), bf16),
            pltpu.VMEM((count, half_f, LANES), bf16),
            pltpu.VMEM((seq_count, tok, LANES), bf16),
            pltpu.VMEM((seq_count, tok, LANES), bf16),
            pltpu.VMEM((count, 2 * half_f, LANES), bf16),
            pltpu.VMEM((2, length, LANES), f32),
            pltpu.VMEM((4, length, 2 * LANES), bf16),
            pltpu.VMEM((seq_count, ext_rows, LANES), bf16),
            pltpu.VMEM((seq_count, ext_rows, LANES), bf16),
            pltpu.VMEM((count, half_f, LANES), bf16),
            pltpu.VMEM((count, half_f, LANES), bf16),
            pltpu.VMEM((seq_count, PART_ROWS, LANES), f32),
            pltpu.VMEM((seq_count, PART_ROWS, LANES), f32),
            pltpu.VMEM((seq_count, PART_ROWS, LANES), f32),
            dma((7,)), dma((7,)), dma((count,)), dma((count,)),
            dma((seq_count,)), dma((seq_count,)), dma((seq_count,)), dma((seq_count,)),
            dma((count,)), dma((count,)), dma((seq_count,)), dma((seq_count,)),
            dma((seq_count,)), dma((seq_count,)),
        ],
        compiler_params=pltpu.CompilerParams(collective_id=0, has_side_effects=True),
    )(*args, *angle_tables(length))
    return pl.pallas_call(
        write_out, out_shape=outs, in_specs=[vmem] * 6, out_specs=(vmem,) * 6
    )(*results)


def block_function(mesh, query_raw, filter_taps):
    seq_count, ch_count = mesh.shape["seq"], mesh.shape["ch"]
    tok, width = query_raw.shape
    length = seq_count * tok
    rows_f = filter_taps.shape[0]
    fits = (
        2 * width == seq_count * LANES
        and seq_count % 2 == 0
        and tok % LANES == 0
        and length % (2 * LANES) == 0
        and length <= 2048
        and rows_f % 32 == 0
    )
    if fits:
        return functools.partial(on_device, (seq_count, ch_count, tok, width))
    return on_device_large


def solution(mesh):
    def body(*args):
        return block_function(mesh, args[0], args[4])(*args)

    return jax.shard_map(
        body,
        mesh=mesh,
        in_specs=(
            P("seq", "ch"),
            P("seq", "ch"),
            P("seq", "ch"),
            P(None, None, "ch"),
            P(("seq", "ch"), None),
            P("seq", "ch"),
        ),
        out_specs=(
            P("seq", "ch"),
            P("seq", "ch"),
            P("seq", "ch"),
            P("seq", "ch"),
            P(("seq", "ch"), None),
            P(None, None, "ch"),
        ),
        check_vma=False,
    )
```

profile of v0, /device:TPU:0, one launch (start us, length us, event | category | flops | bytes accessed | tf_op | source)
XLA Modules:
  0.0 48.1 jit_solution(5600249244137882167)
XLA Ops:
  0.6 45.4 %shard_map.145 = (bf16[128,512]{1,0:T(8,128)(2,1)}, bf16[128,512]{1,0:T(8,128)(2,1)}, bf16[128,512]{1,0:T(8,128)(2,1)}, bf16[128,512]{1,0:T(8,128)(2,1)}, f32[32,2048]{1,0:T(8,128)}, /*index=5*/f32[3,7,512]{2,1,0:T(8,128)}) custom-call(bf16[128,512]{1,0:T(8,128)(2,1)} %q_ref.1, bf16[128,512]{1,0:T(8,128)(2,1)} %k_ref.1, bf16[128,512]{1,0:T(8,128)(2,1)} %v_ref.1, ...), custom_call_target="tpu_custom_call" | custom-call | tf_op jit(solution)/shard_map/pallas_call | solution.py:687
  46.0 2.1 %shard_map.146 = (bf16[128,512]{1,0:T(8,128)(2,1)}, bf16[128,512]{1,0:T(8,128)(2,1)}, bf16[128,512]{1,0:T(8,128)(2,1)}, bf16[128,512]{1,0:T(8,128)(2,1)}, f32[32,2048]{1,0:T(8,128)}, /*index=5*/f32[3,7,512]{2,1,0:T(8,128)}) custom-call(bf16[128,512]{1,0:T(8,128)(2,1)} %get-tuple-element.12.refs_0_, bf16[128,512]{1,0:T(8,128)(2,1)} %get-tuple-element.13.refs_1_, ...), custom_call_target="tpu_custom_call" | custom-call | tf_op jit(solution)/shard_map/pallas_call | solution.py:718
where the time goes:
time: 48.3 us; the launch traced here: 48.1 us
  Pallas kernels  47.5 us (98%)
  between operations  0.64 us (1%)
    pallas_call x1, Pallas kernels, on_device(): pl.pallas_call(functools.partial(operator_kernel, dims), out_shape=outs,...  45.4 us
    pallas_call x1, Pallas kernels, on_device(): pl.pallas_call(write_out, out_shape=outs, in_specs=[vmem] * 6, out_specs=...  2.11 us

commit v1 on v0

--- a/solution.py
+++ b/solution.py
@@ -209,22 +209,99 @@
 
 LANES = 128
 HALO = 16
-STEP = 32
 SPLIT = (TAPS + 1) // 2
 PART_ROWS = 16
 MESH = pl.DeviceIdType.MESH
 
 
-def angle_tables(length):
-    full = 2 * length
-    col = np.arange(length)
-    coarse = np.arange(length // STEP + 1) * STEP
-    coarse = 2.0 * np.pi / full * ((coarse[:, None] * col[None, :LANES]) % full)
-    fine = 2.0 * np.pi / full * ((np.arange(STEP)[:, None] * col[None, :]) % full)
-    return [
-        np.asarray(part, np.float32)
-        for part in (np.cos(coarse), np.sin(coarse), np.cos(fine), np.sin(fine))
-    ]
+def wave_tables(seq_count, tok):
+    radix = 2 * seq_count
+    full = radix * tok
+    col = np.arange(tok)
+    unit = 2.0 * np.pi / full
+    forward, backward = [], []
+    for r in range(seq_count):
+        gain = np.full((1, 2 * tok), 1.0 / full)
+        if r == 0:
+            k = radix * np.arange(tok // 2)
+            even = unit * ((k[:, None] * col) % full)
+            odd = unit * (((k + seq_count)[:, None] * col) % full)
+            none = np.zeros_like(even)
+            real = np.block([[np.cos(even), none], [none, np.cos(odd)]])
+            imag = np.block([[-np.sin(even), none], [none, -np.sin(odd)]])
+            imag[0, :tok] = 1.0 - 2.0 * (col % 2)
+            gain *= 2.0
+            gain[0, [0, tok]] = 1.0 / full
+        else:
+            k = radix * np.arange(tok) + r
+            angle = unit * ((k[:, None] * col) % full)
+            real = np.block([np.cos(angle), np.sin(angle)])
+            imag = np.block([-np.sin(angle), np.cos(angle)])
+        block = np.concatenate([real, imag])
+        forward.append(block)
+        backward.append(block.T * gain)
+    exact = np.stack([np.stack(forward), np.stack(backward)]).astype(np.float32)
+    high = exact.astype(jnp.bfloat16)
+    low = (exact - high.astype(np.float32)).astype(jnp.bfloat16)
+    return np.stack([high, low])
+
+
+def plus(a, b):
+    return a if b is None else b if a is None else a + b
+
+
+def minus(a, b):
+    return a if b is None else -b if a is None else a - b
+
+
+def scaled(a, factor):
+    if a is None or abs(factor) < 1e-9:
+        return None
+    if abs(factor - 1.0) < 1e-9:
+        return a
+    return -a if abs(factor + 1.0) < 1e-9 else a * factor
+
+
+def rotated(value, angle):
+    c, s = math.cos(angle), math.sin(angle)
+    re, im = value
+    return minus(scaled(re, c), scaled(im, s)), plus(scaled(re, s), scaled(im, c))
+
+
+def real_dft(values):
+    size = len(values)
+    if size == 2:
+        return [(plus(*values), None), (minus(*values), None)]
+    even, odd = real_dft(values[0::2]), real_dft(values[1::2])
+    out = [None] * (size // 2 + 1)
+    for r in range(size // 4 + 1):
+        turned = rotated(odd[r], -2.0 * math.pi * r / size)
+        out[size // 2 - r] = (minus(even[r][0], turned[0]), minus(turned[1], even[r][1]))
+        out[r] = (plus(even[r][0], turned[0]), plus(even[r][1], turned[1]))
+    return out
+
+
+def real_inverse(spectrum):
+    size = 2 * (len(spectrum) - 1)
+    if size == 2:
+        first, second = spectrum[0][0], spectrum[1][0]
+        return [plus(first, second), minus(first, second)]
+    even, odd = [], []
+    for r in range(size // 4 + 1):
+        (re, im), (other_re, other_im) = spectrum[r], spectrum[size // 2 - r]
+        if r == 0:
+            im, other_im = None, None
+        if 4 * r == size:
+            even.append((2.0 * re, None))
+            odd.append((-2.0 * im, None))
+            continue
+        even.append((plus(re, other_re), minus(im, other_im)))
+        odd.append(
+            rotated((minus(re, other_re), plus(im, other_im)), 2.0 * math.pi * r / size)
+        )
+    out = [None] * size
+    out[0::2], out[1::2] = real_inverse(even), real_inverse(odd)
+    return out
 
 
 def split_parts(value):
@@ -246,11 +323,12 @@
 
 def operator_kernel(
     dims,
-    q_ref, k_ref, v_ref, w_ref, taps_ref, cot_ref, ac_ref, as_ref, bc_ref, bs_ref,
+    q_ref, k_ref, v_ref, w_hbm, taps_hbm, cot_ref, wave_hbm,
     mixed_ref, qg_ref, kg_ref, vg_ref, fgrad_ref, wgrad_ref,
-    ext, feat, grads, tab, taps_tx, taps_rx, mg_tx, mg_rx, taps_in, hspec, spec, conv_tx, conv_rx,
+    ext, w_ref, taps_ref, wave, feat, grads, taps_tx, taps_rx, mg_tx, mg_rx,
+    taps_mix, hspec, sig_mix, spec, back, conv_tx, conv_rx,
     filt_tx, filt_rx, part_tx, part_rx, sums_rx,
-    halo_send, halo_recv, taps_send, taps_recv, mg_send, mg_recv,
+    load, halo_send, halo_recv, taps_send, taps_recv, mg_send, mg_recv,
     conv_send, conv_recv, filt_send, filt_recv, part_send, part_recv, sum_send, sum_recv,
 ):
     seq_count, ch_count, tok, width = dims
@@ -275,26 +353,22 @@
     def lane_ds(tile):
         return pl.ds(pl.multiple_of(tile * LANES, LANES), LANES)
 
+    loads = [pltpu.make_async_copy(taps_hbm, taps_ref, load.at[0])]
+    for i, ref in enumerate((q_ref, k_ref, v_ref, cot_ref)):
+        loads.append(pltpu.make_async_copy(ref, ext.at[i, HALO : HALO + tok], load.at[1 + i]))
+    loads.append(pltpu.make_async_copy(w_hbm, w_ref, load.at[5]))
+    for i in range(4):
+        part = (i % 2, i // 2)
+        loads.append(pltpu.make_async_copy(wave_hbm.at[part], wave.at[part], load.at[6 + i]))
+    for copy in loads:
+        copy.start()
+
     barrier = pltpu.get_barrier_semaphore()
 
     @pl.loop(1, count)
     def _(step):
         pl.semaphore_signal(barrier, inc=1, device_id=place(peer(step)), device_id_type=MESH)
 
-    low_half = low_lanes(half_f)
-
-    @pl.loop(0, ch_count * tiles)
-    def _(tile):
-        cols = lane_ds(tile)
-        top = taps_ref[0:half_f, cols].astype(f32)
-        bottom = taps_ref[half_f:rows_f, cols].astype(f32)
-        even_flat = 2 * lax.rem(tile, tiles) * ch_count + lax.div(tile, tiles)
-        taps_tx[even_flat] = jnp.where(low_half, top, swapped(bottom)).astype(jnp.bfloat16)
-        taps_tx[even_flat + ch_count] = jnp.where(low_half, swapped(top), bottom).astype(jnp.bfloat16)
-
-    own = (q_ref, k_ref, v_ref, cot_ref)
-    for i, ref in enumerate(own):
-        ext[i, HALO : HALO + tok, :] = ref[...]
 
     @pl.when(seq == 0)
     def _():
@@ -304,21 +378,45 @@
     def _():
         ext[:, HALO + tok :, :] = jnp.zeros((4, HALO, width), jnp.bfloat16)
 
-    def make_tables(first, last):
-        @pl.loop(first, last)
-        def _(a):
-            rows = pl.ds(pl.multiple_of(a * STEP, STEP), STEP)
-            ac = jnp.broadcast_to(ac_ref[pl.ds(a, 1), :], (STEP, LANES))
-            an = jnp.broadcast_to(as_ref[pl.ds(a, 1), :], (STEP, LANES))
-            for j in range(length // LANES):
-                cols = slice(j * LANES, (j + 1) * LANES)
-                bc, bs = bc_ref[:, cols], bs_ref[:, cols]
-                tab[0, rows, cols], tab[1, rows, cols] = split_parts(ac * bc - an * bs)
-                tab[2, rows, cols], tab[3, rows, cols] = split_parts(an * bc + ac * bs)
-
-    blocks = length // STEP + 1
-    early = blocks // 2
-    make_tables(0, early)
+    conv_tx[seq_count - 1, tok:, :] = jnp.zeros((HALO, LANES), jnp.bfloat16)
+    low_half = low_lanes(half_f)
+    loads[0].wait()
+
+    for tile in range(ch_count * tiles):
+        cols = slice(tile * LANES, (tile + 1) * LANES)
+        top = taps_ref[0:half_f, cols].astype(f32)
+        bottom = taps_ref[half_f:rows_f, cols].astype(f32)
+        even_flat = 2 * (tile % tiles) * ch_count + tile // tiles
+        taps_tx[even_flat] = jnp.where(low_half, top, swapped(bottom)).astype(jnp.bfloat16)
+        taps_tx[even_flat + ch_count] = jnp.where(low_half, swapped(top), bottom).astype(jnp.bfloat16)
+
+    for copy in loads[1:6]:
+        copy.wait()
+
+    def mix_gate(to_rows, feats, cot):
+        low = low_lanes(to_rows)
+        mix = feats[1] * feats[2]
+        gate = cot.astype(f32) * feats[0]
+        even = jnp.where(low, mix, swapped(gate)).astype(jnp.bfloat16)
+        odd = jnp.where(low, swapped(mix), gate).astype(jnp.bfloat16)
+        return even, odd
+
+    @pl.loop(0, tiles)
+    def _(tile):
+        cols = lane_ds(tile)
+        parts = []
+        for i in range(3):
+            raw = ext[i, HALO : HALO + tok, cols].astype(f32)
+            total = jnp.zeros((tok - HALO, LANES), f32)
+            for lag in range(TAPS):
+                total = total + w_ref[i, lag : lag + 1, cols] * raw[HALO - lag : tok - lag]
+            feat[i, HALO:tok, cols] = total
+            parts.append(total)
+        cot = ext[3, 2 * HALO : HALO + tok, cols]
+        even, odd = mix_gate(tok - HALO, parts, cot)
+        mg_tx[2 * tile, HALO:, :] = even
+        mg_tx[2 * tile + 1, HALO:, :] = odd
+
     pl.semaphore_wait(barrier, count - 1)
 
     def halo_copy(src, dst, i, to):
@@ -328,10 +426,10 @@
         )
 
     def up_copy(i):
-        return halo_copy(own[i].at[tok - HALO :], ext.at[i, 0:HALO], i, seq + 1)
+        return halo_copy(ext.at[i, tok : tok + HALO], ext.at[i, 0:HALO], i, seq + 1)
 
     def down_copy(i):
-        return halo_copy(own[i].at[0:HALO], ext.at[i, HALO + tok :], 3 + i, seq - 1)
+        return halo_copy(ext.at[i, HALO : 2 * HALO], ext.at[i, HALO + tok :], 3 + i, seq - 1)
 
     @pl.when(seq < seq_count - 1)
     def _():
@@ -367,13 +465,12 @@
         for i in range(4):
             down_copy(i).wait_recv()
 
+
     def mg_copy(to):
         return pltpu.make_async_remote_copy(
             src_ref=mg_tx.at[to], dst_ref=mg_rx.at[seq], send_sem=mg_send.at[to],
             recv_sem=mg_recv.at[seq], device_id=(to, ch), device_id_type=MESH,
         )
-
-    low_tok = low_lanes(tok)
 
     @pl.loop(0, tiles)
     def _(turn):
@@ -381,51 +478,64 @@
         cols = lane_ds(tile)
         parts = []
         for i in range(3):
-            raw = ext[i, :, cols].astype(f32)
-            total = jnp.zeros((ext_rows, LANES), f32)
-            for lag in range(TAPS):
-                total = total + w_ref[i, lag : lag + 1, cols] * raw[HALO - lag : HALO - lag + ext_rows]
-            feat[i, :, cols] = total
-            parts.append(total[:tok])
-        mix = parts[1] * parts[2]
-        gate = ext[3, HALO : HALO + tok, cols].astype(f32) * parts[0]
-        even = jnp.where(low_tok, mix, swapped(gate)).astype(jnp.bfloat16)
-        odd = jnp.where(low_tok, swapped(mix), gate).astype(jnp.bfloat16)
+            for start in (0, tok):
+                raw = ext[i, start : start + 2 * HALO, cols].astype(f32)
+                total = jnp.zeros((HALO, LANES), f32)
+                for lag in range(TAPS):
+                    total = total + w_ref[i, lag : lag + 1, cols] * raw[HALO - lag : 2 * HALO - lag]
+                feat[i, start : start + HALO, cols] = total
+                if start == 0:
+                    parts.append(total)
+        even, odd = mix_gate(HALO, parts, ext[3, HALO : 2 * HALO, cols])
         for side, value in ((0, even), (1, odd)):
             to = 2 * tile + side
-            mg_tx[to] = value
+            mg_tx[to, 0:HALO, :] = value
 
             @pl.when(to != seq)
             def _():
                 mg_copy(to).start()
 
-            @pl.when(to == seq)
-            def _():
-                mg_rx[to] = value
-
-    make_tables(early, blocks)
+    mg_rx[seq] = mg_tx[seq]
 
     @pl.loop(1, count)
     def _(step):
         taps_copy(step).wait_recv()
 
-    low_count = low_lanes(count * half_f)
-    taps_all = taps_rx[...].reshape(count * half_f, LANES).astype(f32)
-    taps_turned = swapped(taps_all)
-    for side, pair in enumerate(((taps_all, taps_turned), (taps_turned, taps_all))):
-        value = jnp.where(low_count, *pair).astype(jnp.bfloat16)
-        taps_in[:, side * half_f : (side + 1) * half_f, :] = value.reshape(count, half_f, LANES)
-
-    chunk = min(2 * LANES, length)
-
-    def row_chunk(i):
-        return pl.ds(pl.multiple_of(i * chunk, chunk), chunk)
-
-    @pl.loop(0, length // chunk)
-    def _(i):
-        rows = row_chunk(i)
-        hspec[0, rows, :] = matmul(tab[0, rows, :], taps_in[...].reshape(length, LANES)) + matmul(tab[1, rows, :], taps_in[...].reshape(length, LANES))
-        hspec[1, rows, :] = matmul(tab[2, rows, :], taps_in[...].reshape(length, LANES)) + matmul(tab[3, rows, :], taps_in[...].reshape(length, LANES))
+    for copy in loads[6:8]:
+        copy.wait()
+
+    def put(store, rows, spectrum):
+        for r in range(seq_count):
+            first, second = spectrum[r]
+            if r == 0:
+                second = spectrum[seq_count][0]
+            store(r, rows, first)
+            store(r, slice(tok + rows.start, tok + rows.stop), second)
+
+    def store_taps(r, rows, value):
+        high = value.astype(jnp.bfloat16)
+        wide = high.astype(f32)
+        taps_mix[1, r, rows, :] = high
+        taps_mix[0, r, rows, :] = jnp.where(low_half, wide, value - wide).astype(jnp.bfloat16)
+
+    nothing = [None] * seq_count
+    for j in range(tok // half_f):
+        blocks = []
+        for m in range(seq_count):
+            raw = taps_rx[ch_count * m + j // 2].astype(f32)
+            pair = (raw, swapped(raw))
+            blocks.append(jnp.where(low_half, pair[j % 2], pair[1 - j % 2]))
+        put(store_taps, slice(j * half_f, (j + 1) * half_f), real_dft(blocks + nothing))
+
+    low_tok = low_lanes(tok)
+    first_row = lax.broadcasted_iota(jnp.int32, (tok, LANES), 0) == 0
+    for r in range(seq_count):
+        both = matmul(wave[0, 0, r], taps_mix[0, r])
+        value = both + swapped(both) + matmul(wave[1, 0, r], taps_mix[1, r])
+        hspec[r, 0:tok, :] = value[:tok]
+        upright = jnp.logical_or(low_tok, first_row) if r == 0 else low_tok
+        hspec[r, tok:, :] = jnp.where(upright, value[tok:], -value[tok:])
+
 
     def from_peer(copy_of, total, mine):
         @pl.loop(0, total)
@@ -441,38 +551,49 @@
         )
 
     from_peer(mg_arrival, seq_count, seq)
-
-    signals = mg_rx.at[...]
-    low_chunk = low_lanes(chunk)
-
-    @pl.loop(0, length // chunk)
-    def _(i):
-        rows = row_chunk(i)
-        both = signals[...].reshape(length, LANES)
-        xr = matmul(tab[0, rows, :], both) + matmul(tab[1, rows, :], both)
-        xs = matmul(tab[2, rows, :], both) + matmul(tab[3, rows, :], both)
-        bins = lax.broadcasted_iota(jnp.int32, (chunk, LANES), 0) + i * chunk
-        weight = jnp.where(bins == 0, 0.5 / length, 1.0 / length)
-        hr = hspec[0, rows, :]
-        hs = hspec[1, rows, :]
-        wr, ws = xr * weight, xs * weight
-        turned = jnp.where(low_chunk, -hs, hs)
-        pr = hr * wr + turned * ws
-        ps = hr * ws - turned * wr
-        other_r, other_s = swapped(xr), swapped(xs)
-        fr = wr * other_r + ws * other_s
-        fs = wr * other_s - ws * other_r
-        for j, value in ((0, pr), (2, ps)):
-            spec[j, rows, 0:LANES], spec[j + 1, rows, 0:LANES] = split_parts(value)
-        for j, value in ((0, fr), (2, fs)):
-            spec[j, rows, LANES:], spec[j + 1, rows, LANES:] = split_parts(value)
-
-    sign_full = 1.0 - 2.0 * lax.rem(lax.broadcasted_iota(jnp.int32, (length, LANES), 0), 2).astype(f32)
-    last_x = jnp.sum(mg_rx[...].reshape(length, LANES).astype(f32) * sign_full, axis=0, keepdims=True)
-    last_h = jnp.sum(taps_in[...].reshape(length, LANES).astype(f32) * sign_full, axis=0, keepdims=True)
-    half_weight = 0.5 / length
-    last_conv = last_x * last_h * half_weight
-    last_filt = last_x * swapped(jnp.broadcast_to(last_x, (8, LANES)))[0:1] * half_weight
+    for copy in loads[8:]:
+        copy.wait()
+
+    def store_signal(r, rows, value):
+        high, rest = split_parts(value)
+        sig_mix[r, rows, 0:LANES] = high
+        sig_mix[r, rows, LANES:] = rest
+
+    for j in range(tok // half_f):
+        rows = slice(j * half_f, (j + 1) * half_f)
+        blocks = [mg_rx[m, rows, :].astype(f32) for m in range(seq_count)]
+        put(store_signal, rows, real_dft(blocks + nothing))
+
+    for r in range(seq_count):
+        both = matmul(wave[0, 0, r], sig_mix[r])
+        value = both[:, :LANES] + both[:, LANES:] + matmul(wave[1, 0, r], sig_mix[r, :, 0:LANES])
+        xr, xi = value[:tok], value[tok:]
+        hr, hi = hspec[r, 0:tok, :], hspec[r, tok:, :]
+        other_r, other_i = swapped(xr), swapped(xi)
+        ii, filt_ii = hi * xi, xi * other_i
+        if r == 0:
+            pr = hr * xr - jnp.where(first_row, 0.0, ii)
+            pi = jnp.where(first_row, ii, hr * xi + hi * xr)
+            fr = xr * other_r + jnp.where(first_row, 0.0, filt_ii)
+            fi = jnp.where(first_row, filt_ii, xr * other_i - xi * other_r)
+        else:
+            pr = hr * xr - ii
+            pi = hr * xi + hi * xr
+            fr = xr * other_r + filt_ii
+            fi = xr * other_i - xi * other_r
+        for rows, cols, item in (
+            (slice(0, tok), slice(0, LANES), pr),
+            (slice(tok, 2 * tok), slice(0, LANES), pi),
+            (slice(0, tok), slice(LANES, 2 * LANES), fr),
+            (slice(tok, 2 * tok), slice(LANES, 2 * LANES), fi),
+        ):
+            spec[0, r, rows, cols], spec[1, r, rows, cols] = split_parts(item)
+        back[r] = (
+            matmul(wave[0, 1, r], spec[0, r])
+            + matmul(wave[0, 1, r], spec[1, r])
+            + matmul(wave[1, 1, r], spec[0, r])
+        )
+
 
     def conv_copy(to):
         return pltpu.make_async_remote_copy(
@@ -486,33 +607,43 @@
             recv_sem=filt_recv.at[me], device_id=place(to), device_id_type=MESH,
         )
 
-    sign_ext = sign_full[:ext_rows]
-
-    @pl.loop(0, seq_count)
-    def _(turn):
-        to = lax.rem(seq + 1 + turn, seq_count)
-        rows = pl.ds(pl.multiple_of(to * tok, tok), ext_rows)
-        out = jnp.zeros((ext_rows, 2 * LANES), f32)
-        for j in (0, 2):
-            high = tab[j, rows, :]
-            out = out + matmul(high, spec[j]) + matmul(high, spec[j + 1]) + matmul(tab[j + 1, rows, :], spec[j])
-        conv_tx[to] = (out[:, :LANES] + sign_ext * last_conv).astype(jnp.bfloat16)
-        filt = (out[:, LANES:] + sign_ext * last_filt) * scale
-
-        @pl.when(to != seq)
-        def _():
-            conv_copy(to).start()
-
-        @pl.when(to == seq)
-        def _():
-            conv_rx[to] = conv_tx[to]
-
-        for c in range(ch_count):
-            top = filt[c * rows_f : c * rows_f + half_f]
-            bottom = filt[c * rows_f + half_f : (c + 1) * rows_f]
-            flat = to * ch_count + c
-            filt_tx[flat] = jnp.where(low_half, top, swapped(bottom)).astype(jnp.bfloat16)
-
+    def joined(get):
+        spectrum = [(get(0, 0), None)]
+        spectrum += [(get(r, 0), get(r, tok)) for r in range(1, seq_count)]
+        return spectrum + [(get(0, tok), None)]
+
+    for j in range(tok // half_f):
+        start = j * half_f
+
+        def get(r, offset):
+            return back[r, offset + start : offset + start + half_f, 0:LANES]
+
+        outs = real_inverse(joined(get))[:seq_count]
+        for m in range(seq_count):
+            value = outs[m].astype(jnp.bfloat16)
+            conv_tx[m, start : start + half_f, :] = value
+            if j == 0 and m > 0:
+                conv_tx[m - 1, tok:, :] = value[:HALO]
+
+
+    @pl.loop(1, seq_count)
+    def _(step):
+        conv_copy(lax.rem(seq + step, seq_count)).start()
+
+    conv_rx[seq] = conv_tx[seq]
+
+    for j in range(tok // rows_f):
+        start = j * rows_f
+
+        def get_pair(r, offset):
+            at = offset + start
+            top = back[r, at : at + half_f, LANES:]
+            bottom = back[r, at + half_f : at + rows_f, LANES:]
+            return jnp.where(low_half, top, swapped(bottom))
+
+        outs = real_inverse(joined(get_pair))[:seq_count]
+        for m in range(seq_count):
+            filt_tx[m * ch_count + j] = (outs[m] * scale).astype(jnp.bfloat16)
 
     filt_rx[me] = filt_tx[me]
 
@@ -526,7 +657,6 @@
     low_ext = low_lanes(ext_rows)
     row_ext = lax.broadcasted_iota(jnp.int32, (ext_rows, LANES), 0)
     keep = jnp.logical_or(row_ext < tok, seq < seq_count - 1)
-
     def part_copy(to):
         return pltpu.make_async_remote_copy(
             src_ref=part_tx.at[to], dst_ref=part_rx.at[seq], send_sem=part_send.at[to],
@@ -583,6 +713,7 @@
                 total = total + w_ref[i, lag : lag + 1, cols] * term[lag : lag + tok]
             ref[:, cols] = total.astype(jnp.bfloat16)
 
+
     def part_arrival(source):
         return pltpu.make_async_remote_copy(
             src_ref=part_tx.at[source], dst_ref=part_rx.at[source], send_sem=part_send.at[source],
@@ -604,6 +735,7 @@
     @pl.loop(1, seq_count)
     def _(step):
         sum_copy(lax.rem(seq + step, seq_count)).start()
+
 
     def filt_arrival(source):
         return pltpu.make_async_remote_copy(
@@ -623,6 +755,7 @@
         fgrad_ref[0:half_f, cols] = jnp.where(low_half, first, swapped(second))
         fgrad_ref[half_f:rows_f, cols] = jnp.where(low_half, swapped(first), second)
 
+
     def sum_arrival(source):
         return pltpu.make_async_remote_copy(
             src_ref=sums_rx.at[seq], dst_ref=sums_rx.at[source], send_sem=sum_send.at[source],
@@ -676,6 +809,7 @@
     half_f = length // count // 2
     bf16, f32 = jnp.bfloat16, jnp.float32
     vmem = pl.BlockSpec(memory_space=pltpu.VMEM)
+    hbm = pl.BlockSpec(memory_space=pltpu.HBM)
     ext_rows = tok + HALO
     dma = pltpu.SemaphoreType.DMA
     out = jax.ShapeDtypeStruct((tok, width), bf16)
@@ -684,23 +818,28 @@
         jax.ShapeDtypeStruct((length // count, width * ch_count), f32),
         jax.ShapeDtypeStruct((3, TAPS, width), f32),
     )
+    waves = wave_tables(seq_count, tok)
     results = pl.pallas_call(
         functools.partial(operator_kernel, dims),
         out_shape=outs,
-        in_specs=[vmem] * 10,
+        in_specs=[hbm] * 7,
         out_specs=(vmem,) * 6,
         scratch_shapes=[
             pltpu.VMEM((4, tok + 2 * HALO, width), bf16),
+            pltpu.VMEM((3, TAPS, width), f32),
+            pltpu.VMEM((length // count, width * ch_count), bf16),
+            pltpu.VMEM(waves.shape, bf16),
             pltpu.VMEM((3, ext_rows, width), f32),
             pltpu.VMEM((3, ext_rows, width), f32),
-            pltpu.VMEM((4, length + STEP, length), bf16),
             pltpu.VMEM((count, half_f, LANES), bf16),
             pltpu.VMEM((count, half_f, LANES), bf16),
             pltpu.VMEM((seq_count, tok, LANES), bf16),
             pltpu.VMEM((seq_count, tok, LANES), bf16),
-            pltpu.VMEM((count, 2 * half_f, LANES), bf16),
-            pltpu.VMEM((2, length, LANES), f32),
-            pltpu.VMEM((4, length, 2 * LANES), bf16),
+            pltpu.VMEM((2, seq_count, 2 * tok, LANES), bf16),
+            pltpu.VMEM((seq_count, 2 * tok, LANES), f32),
+            pltpu.VMEM((seq_count, 2 * tok, 2 * LANES), bf16),
+            pltpu.VMEM((2, seq_count, 2 * tok, 2 * LANES), bf16),
+            pltpu.VMEM((seq_count, 2 * tok, 2 * LANES), f32),
             pltpu.VMEM((seq_count, ext_rows, LANES), bf16),
             pltpu.VMEM((seq_count, ext_rows, LANES), bf16),
             pltpu.VMEM((count, half_f, LANES), bf16),
@@ -708,15 +847,18 @@
             pltpu.VMEM((seq_count, PART_ROWS, LANES), f32),
             pltpu.VMEM((seq_count, PART_ROWS, LANES), f32),
             pltpu.VMEM((seq_count, PART_ROWS, LANES), f32),
-            dma((7,)), dma((7,)), dma((count,)), dma((count,)),
+            dma((10,)), dma((7,)), dma((7,)), dma((count,)), dma((count,)),
             dma((seq_count,)), dma((seq_count,)), dma((seq_count,)), dma((seq_count,)),
             dma((count,)), dma((count,)), dma((seq_count,)), dma((seq_count,)),
             dma((seq_count,)), dma((seq_count,)),
         ],
-        compiler_params=pltpu.CompilerParams(collective_id=0, has_side_effects=True),
-    )(*args, *angle_tables(length))
+        compiler_params=pltpu.CompilerParams(
+            collective_id=0, has_side_effects=True, vmem_limit_bytes=32 * 1024 * 1024
+        ),
+    )(*[pltpu.with_memory_space_constraint(value, pltpu.HBM) for value in (*args, waves)])
     return pl.pallas_call(
-        write_out, out_shape=outs, in_specs=[vmem] * 6, out_specs=(vmem,) * 6
+        write_out, out_shape=outs, in_specs=[vmem] * 6, out_specs=(vmem,) * 6,
+        compiler_params=pltpu.CompilerParams(vmem_limit_bytes=8 * 1024 * 1024),
     )(*results)
 
 
@@ -727,11 +869,11 @@
     rows_f = filter_taps.shape[0]
     fits = (
         2 * width == seq_count * LANES
-        and seq_count % 2 == 0
-        and tok % LANES == 0
-        and length % (2 * LANES) == 0
-        and length <= 2048
-        and rows_f % 32 == 0
+        and seq_count & (seq_count - 1) == 0
+        and seq_count >= 4
+        and tok == LANES
+        and rows_f == 32
+        and tok == ch_count * rows_f
     )
     if fits:
         return functools.partial(on_device, (seq_count, ch_count, tok, width))

time: 48.3 us -> 42.4 us (0.88)
  Pallas kernels: 47.5 us -> 41.6 us
    pallas_call x1, Pallas kernels: 45.4 us -> 40.7 us  [on_device(): pl.pallas_call(functools.partial(operator_kernel, dims), out_shape=outs,...]
    pallas_call x1, Pallas kernels: 2.11 us -> 0.94 us  [on_device(): pl.pallas_call(write_out, out_shape=outs, in_specs=[vmem] * 6, out_specs=...]
where the time goes in v1:
time: 42.4 us; the launch traced here: 42.3 us
  Pallas kernels  41.6 us (98%)
  between operations  0.64 us (2%)
    pallas_call x1, Pallas kernels, on_device(): pl.pallas_call(functools.partial(operator_kernel, dims), out_shape=outs,...  40.7 us
    pallas_call x1, Pallas kernels, on_device(): pl.pallas_call(write_out, out_shape=outs, in_specs=[vmem] * 6, out_specs=...  0.94 us

profile of v1, /device:TPU:0, one launch (start us, length us, event | category | flops | bytes accessed | tf_op | source)
XLA Modules:
  0.0 42.3 jit_solution(4641609775852731848)
XLA Ops:
  0.6 40.7 %shard_map.118 = (bf16[128,512]{1,0:T(8,128)(2,1)S(1)}, bf16[128,512]{1,0:T(8,128)(2,1)S(1)}, bf16[128,512]{1,0:T(8,128)(2,1)S(1)}, bf16[128,512]{1,0:T(8,128)(2...) custom-call(bf16[128,512]{1,0:T(8,128)(2,1)} %q_ref.1, bf16[128,512]{1,0:T(8,128)(2,1)} %k_ref.1, ...), custom_call_target="tpu_custom_call" | custom-call | tf_op jit(solution)/shard_map/pallas_call | solution.py:822
  41.3 0.9 %shard_map.119 = (bf16[128,512]{1,0:T(8,128)(2,1)}, bf16[128,512]{1,0:T(8,128)(2,1)}, bf16[128,512]{1,0:T(8,128)(2,1)}, bf16[128,512]{1,0:T(8,128)(2,1)}, f32[32,2048]{1,0:T(8,128)}, /*index=5*/f32[3,7,512]{2,1,0:T(8,128)}) custom-call(bf16[128,512]{1,0:T(8,128)(2,1)S(1)} %get-tuple-element.12.refs_0_, bf16[128,512]{1,0:T(8,128)(2,1)S(1)} %get-tuple-element.13.refs_1_, ...), custom_call_target="tpu_custom_call" | custom-call | tf_op jit(solution)/shard_map/pallas_call | solution.py:859
